TPU v7x, 32 devices: a whole 2x2x4 slice. The times are simulated.
32 devices in a mesh: groups: 2 (over y), chan: 4 (over z), tm: 2 (over x), sub: 2 (over core).
Axes of the slice: x: 2, y: 2, z: 4, core: 2. Of those that a mesh axis runs over, the one named last changes fastest.
Arguments:
- traces: float32 [2048, 8192], P(('groups', 'chan', 'sub'), 'tm'), parts along dimension 0, may hold values from -6 to 6
- filters: float32 [2048, 65], P(('groups', 'chan', 'sub')), parts along dimension 0, may hold values from -0.75 to 0.75
- sources: int32 [256], P('groups'), parts along dimension 0, may hold values from 0 to 1023, as said below
Outputs:
- corr: float32 [128, 129, 2048], P('tm', None, ('groups', 'chan', 'sub')), parts along dimension 2
There are 2 independent parts, one for each index of `groups`. A program takes and returns all parts, laid end to end along the dimension named above; each array names one. Nothing has to cross between parts.
Inputs may be any that keep to these rules, and one draw needn't show every extreme that they name: `sources`: the 128 partner channels are distinct. No block of 128 consecutive channels starting at a multiple of 128 holds more than 16 of them, and some block holds exactly 16.
All inputs are finite; a program needn't handle non-finite values.
Results may differ from a plain program's by a relative error of at most 0.0033.
Values may be sent and summed in bfloat16 or wider, within the bound.
A program may use at most 64 MiB of HBM per device.

v0:
```python
import math

import jax
import jax.numpy as jnp
from jax import lax
from jax.sharding import PartitionSpec as P

LAGS = 129


def padded_2(block, sides, width):
    for axis, dim in sides:
        count = lax.axis_size(axis)
        forward = [(i, i + 1) for i in range(count - 1)]
        backward = [(target, source) for source, target in forward]
        low = lax.ppermute(
            lax.slice_in_dim(block, block.shape[dim] - width, None, axis=dim), axis, forward
        )
        high = lax.ppermute(lax.slice_in_dim(block, 0, width, axis=dim), axis, backward)
        block = jnp.concatenate([low, block, high], axis=dim)
    return block


def whiten(extended, filters, out_len):
    running = jnp.zeros((extended.shape[0], out_len), jnp.float32)
    for k in range(filters.shape[1]):
        running = running + filters[:, k : k + 1] * extended[:, k : k + out_len]
    return running


def correlate(padded_seg, part_rows):
    seg_len = part_rows.shape[1]
    block_len = min(512, seg_len)
    block_count = seg_len // block_len

    def advance(block_index, summed):
        offset = block_index * block_len
        window = lax.dynamic_slice_in_dim(padded_seg, offset, block_len + LAGS - 1, 1)
        rows_here = lax.dynamic_slice_in_dim(part_rows, offset, block_len, 1)
        term = lax.conv_general_dilated(
            window[:, None, :],
            rows_here[:, None, :],
            (1,),
            "VALID",
            dimension_numbers=("NCH", "OIH", "NCH"),
            preferred_element_type=jnp.float32,
        )
        return summed + term

    start_sum = jnp.zeros((padded_seg.shape[0], part_rows.shape[0], LAGS), jnp.float32)
    return lax.fori_loop(0, block_count, advance, start_sum)


def on_device(traces, filters, sources):
    chan_dev, seg_len = traces.shape
    taps = filters.shape[1]
    half_taps = (taps - 1) // 2
    half_lags = (LAGS - 1) // 2
    partner_count = sources.shape[0]
    time_devs = lax.axis_size("tm")
    extended = padded_2(traces, (("tm", 1),), half_taps + half_lags)
    whitened_ext = whiten(extended, filters, seg_len + 2 * half_lags)
    position = (
        lax.axis_index("tm") * seg_len
        - half_lags
        + jnp.arange(seg_len + 2 * half_lags, dtype=jnp.int32)
    )
    inside = (position >= 0) & (position < seg_len * time_devs)
    padded = jnp.where(inside[None, :], whitened_ext, 0.0).astype(jnp.bfloat16)
    whitened = padded[:, half_lags : half_lags + seg_len]
    my_block = lax.axis_index(("chan", "sub"))
    owners = sources // chan_dev
    within = sources % chan_dev
    is_mine = owners == my_block
    chan_ids = jnp.arange(chan_dev, dtype=jnp.int32)
    slot_most = min(chan_dev, partner_count // 8)
    order_ids = jnp.arange(partner_count, dtype=jnp.int32)
    same_owner = owners[:, None] == owners[None, :]
    earlier = order_ids[None, :] < order_ids[:, None]
    rank_in = jnp.sum((same_owner & earlier).astype(jnp.int32), axis=1)
    choose = (
        (rank_in[None, :] == jnp.arange(slot_most, dtype=jnp.int32)[:, None]) & is_mine[None, :]
    ).astype(jnp.bfloat16)
    onehot = (within[:, None] == chan_ids[None, :]).astype(jnp.bfloat16)
    picker = jnp.dot(choose, onehot, preferred_element_type=jnp.float32).astype(jnp.bfloat16)
    slot_rows = jnp.dot(picker, whitened, preferred_element_type=jnp.float32).astype(jnp.bfloat16)
    slot_id = owners * slot_most + rank_in
    segment = lax.all_gather(slot_rows, ("chan", "sub"), axis=0, tiled=True)
    row_count = segment.shape[0]
    select = (slot_id[:, None] == jnp.arange(row_count, dtype=jnp.int32)[None, :]).astype(
        jnp.bfloat16
    )
    partners = jnp.dot(select, segment, preferred_element_type=jnp.float32).astype(jnp.bfloat16)
    norm_scale = 1.0 / math.sqrt(seg_len * time_devs)
    summed = correlate(padded, partners)
    return lax.psum_scatter(
        jnp.transpose(summed[:, :, ::-1], (1, 2, 0)) * norm_scale,
        "tm",
        scatter_dimension=0,
        tiled=True,
    )


def solution(mesh):
    return jax.shard_map(
        on_device,
        mesh=mesh,
        in_specs=(
            P(("groups", "chan", "sub"), "tm"),
            P(("groups", "chan", "sub"), None),
            P("groups"),
        ),
        out_specs=P("tm", None, ("groups", "chan", "sub")),
        check_vma=False,
    )
```

profile of v0, /device:TPU:0, one launch (start us, length us, event | category | flops | bytes accessed | tf_op | source)
XLA Modules:
  0.0 404.3 jit_solution(17135391241325937660)
XLA Ops:
  6.5 1.0 fusion.81
  7.5 1.3 collective-permute-start.1
  8.8 4.9 %collective-permute-start = (f32[128,96]{1,0:T(8,128)S(1)}, f32[128,96]{1,0:T(8,128)S(1)}, u32[]{:S(2)}, u32[]{:S(2)}) collective-permute-start(f32[128,96]{1,0:T(8,128)S(1)} %get-tuple-element.115), channel_id=1, source_target_pairs={{0,2},{1,3},{4,6},{5,7},{8,10},{9,11},{12,14},{13,15},{16,18},{17,... | collective-permute-start | bytes 147464 | tf_op jit(solution)/shard_map/ppermute | solution.py:16
  14.6 1.0 slice_bitcast_fusion.63
  15.6 1.0 slice_bitcast_fusion.64
  16.6 1.0 slice_bitcast_fusion.62
  19.1 2.9 concatenate.3
  22.1 42.9 %fusion.2 = bf16[128,4224]{1,0:T(8,128)(2,1)} fusion(f32[128,4288]{1,0:T(8,128)S(1)} %concatenate.3, f32[128]{0:T(128)S(1)} %get-tuple-element.179, f32[128]{0:T(128)S(1)} %get-tuple-element.180, f32[128]{0:T(128)S(1)} %get-tuple-element.117, f32[128]{0:T(128)S(1)} %get-tuple-element.118, f32[128]{0:T(128)S(1)} %get-tuple-element.119, ...), kind=kLoop, calls=%fused_computation.9 | loop fusion | flops 70828032 | bytes 141693568 | tf_op jit(solution)/shard_map/convert_element_type | solution.py:69
  65.0 2.4 convolution_convert_fusion.1
  67.7 23.6 %all-gather.2.cloned.1.call-done = bf16[128,4096]{1,0:T(8,128)(2,1)} async-done(((bf16[16,4096]{1,0:T(8,128)(2,1)}), bf16[128,4096]{1,0:T(8,128)(2,1)}) %all-gather.2.cloned.1.call-update) | async-done | bytes 1048592 | tf_op jit(solution)/shard_map/all_gather | solution.py:88
  91.3 2.8 convolution_convert_fusion
  94.0 186.1 %while.14 = (s32[]{:T(128)}, f32[128,128,129]{1,0,2:T(8,128)}, bf16[128,4224]{1,0:T(8,128)(2,1)}, bf16[128,4096]{1,0:T(8,128)(2,1)}, s32[]{:T(128)}, /*index=5*/s32[]{:T(128)}, s32[]{:T(128)}, s32[]{:T(128)}, s32[]{:T(128)}) while((s32[]{:T(128)}, f32[128,128,129]{1,0,2:T(8,128)}, bf16[128,4224]{1,0:T(8,128)(2,1)}, ...), condition=%wide.region_2.3_spmd.clone, body=%wide.region_1.2_spmd.clone.sunk | while | flops 2168487936 | bytes 18383036 | solution.py:51
  95.1 0.9 dynamic-slice_bitcast_fusion.4
  96.3 19.1 %select_add_fusion.2 = f32[128,128,129]{1,0,2:T(8,128)} fusion(f32[128,128,129]{1,0,2:T(8,128)} %get-tuple-element.216, pred[]{:T(512)S(6)} %compare.6, bf16[128,1,640]{0,1,2:T(2,128)(2,1)S(1)} %copy.17, bf16[128,1,512]{0,1,2:T(2,128)(2,1)S(1)} %copy.18), kind=kOutput, calls=%fused_computation.clone.1 | convolution fusion | flops 2168487936 | bytes 17203200 | tf_op jit(solution)/shard_map/while/body/eval_jaxpr/conv_general_dilated | solution.py:40
  117.6 21.3 %select_add_fusion.2 = f32[128,128,129]{1,0,2:T(8,128)} fusion(f32[128,128,129]{1,0,2:T(8,128)} %get-tuple-element.216, pred[]{:T(512)S(6)} %compare.6, bf16[128,1,640]{0,1,2:T(2,128)(2,1)S(1)} %copy.17, bf16[128,1,512]{0,1,2:T(2,128)(2,1)S(1)} %copy.18), kind=kOutput, calls=%fused_computation.clone.1 | convolution fusion | flops 2168487936 | bytes 17203200 | tf_op jit(solution)/shard_map/while/body/eval_jaxpr/conv_general_dilated | solution.py:40
  141.2 21.3 %select_add_fusion.2 = f32[128,128,129]{1,0,2:T(8,128)} fusion(f32[128,128,129]{1,0,2:T(8,128)} %get-tuple-element.216, pred[]{:T(512)S(6)} %compare.6, bf16[128,1,640]{0,1,2:T(2,128)(2,1)S(1)} %copy.17, bf16[128,1,512]{0,1,2:T(2,128)(2,1)S(1)} %copy.18), kind=kOutput, calls=%fused_computation.clone.1 | convolution fusion | flops 2168487936 | bytes 17203200 | tf_op jit(solution)/shard_map/while/body/eval_jaxpr/conv_general_dilated | solution.py:40
  164.7 21.3 %select_add_fusion.2 = f32[128,128,129]{1,0,2:T(8,128)} fusion(f32[128,128,129]{1,0,2:T(8,128)} %get-tuple-element.216, pred[]{:T(512)S(6)} %compare.6, bf16[128,1,640]{0,1,2:T(2,128)(2,1)S(1)} %copy.17, bf16[128,1,512]{0,1,2:T(2,128)(2,1)S(1)} %copy.18), kind=kOutput, calls=%fused_computation.clone.1 | convolution fusion | flops 2168487936 | bytes 17203200 | tf_op jit(solution)/shard_map/while/body/eval_jaxpr/conv_general_dilated | solution.py:40
  188.3 21.3 %select_add_fusion.2 = f32[128,128,129]{1,0,2:T(8,128)} fusion(f32[128,128,129]{1,0,2:T(8,128)} %get-tuple-element.216, pred[]{:T(512)S(6)} %compare.6, bf16[128,1,640]{0,1,2:T(2,128)(2,1)S(1)} %copy.17, bf16[128,1,512]{0,1,2:T(2,128)(2,1)S(1)} %copy.18), kind=kOutput, calls=%fused_computation.clone.1 | convolution fusion | flops 2168487936 | bytes 17203200 | tf_op jit(solution)/shard_map/while/body/eval_jaxpr/conv_general_dilated | solution.py:40
  211.8 21.3 %select_add_fusion.2 = f32[128,128,129]{1,0,2:T(8,128)} fusion(f32[128,128,129]{1,0,2:T(8,128)} %get-tuple-element.216, pred[]{:T(512)S(6)} %compare.6, bf16[128,1,640]{0,1,2:T(2,128)(2,1)S(1)} %copy.17, bf16[128,1,512]{0,1,2:T(2,128)(2,1)S(1)} %copy.18), kind=kOutput, calls=%fused_computation.clone.1 | convolution fusion | flops 2168487936 | bytes 17203200 | tf_op jit(solution)/shard_map/while/body/eval_jaxpr/conv_general_dilated | solution.py:40
  235.3 21.3 %select_add_fusion.2 = f32[128,128,129]{1,0,2:T(8,128)} fusion(f32[128,128,129]{1,0,2:T(8,128)} %get-tuple-element.216, pred[]{:T(512)S(6)} %compare.6, bf16[128,1,640]{0,1,2:T(2,128)(2,1)S(1)} %copy.17, bf16[128,1,512]{0,1,2:T(2,128)(2,1)S(1)} %copy.18), kind=kOutput, calls=%fused_computation.clone.1 | convolution fusion | flops 2168487936 | bytes 17203200 | tf_op jit(solution)/shard_map/while/body/eval_jaxpr/conv_general_dilated | solution.py:40
  258.9 21.3 %select_add_fusion.2 = f32[128,128,129]{1,0,2:T(8,128)} fusion(f32[128,128,129]{1,0,2:T(8,128)} %get-tuple-element.216, pred[]{:T(512)S(6)} %compare.6, bf16[128,1,640]{0,1,2:T(2,128)(2,1)S(1)} %copy.17, bf16[128,1,512]{0,1,2:T(2,128)(2,1)S(1)} %copy.18), kind=kOutput, calls=%fused_computation.clone.1 | convolution fusion | flops 2168487936 | bytes 17203200 | tf_op jit(solution)/shard_map/while/body/eval_jaxpr/conv_general_dilated | solution.py:40
  280.2 9.0 %copy.14 = f32[128,128,129]{0,1,2:T(8,128)} copy(f32[128,128,129]{1,0,2:T(8,128)} %get-tuple-element.84) | data formatting | bytes 16908288 | tf_op jit(solution)/shard_map/while | solution.py:51
  289.2 8.5 %multiply_bitcast_fusion = f32[128,129,128]{2,0,1:T(8,128)} fusion(f32[128,128,129]{0,1,2:T(8,128)} %copy.14), kind=kLoop, calls=%fused_computation.3 | loop fusion | flops 2113536 | bytes 16908288 | tf_op jit(solution)/shard_map/mul | solution.py:97
  297.7 99.8 %reduce-scatter.2.cloned.1.call-done = f32[64,129,128]{2,0,1:T(8,128)} async-done(((f32[128,129,128]{2,0,1:T(8,128)}), f32[64,129,128]{2,0,1:T(8,128)}) %reduce-scatter.2.cloned.1.call-update) | async-done | bytes 4227088 | tf_op jit(solution)/shard_map/reduce_scatter | solution.py:96
  (44 shorter events, 19.5 us)
Async XLA Ops:
  6.5 84.7 %all-gather.2.cloned.1.call-start = ((), (), s32[]{:S(2)}) async-start(), calls=%async_computation.1 | async-start | bytes 1179648 | tf_op jit(solution)/shard_map/all_gather | solution.py:88
  7.5 11.6 %collective-permute-start.1 = (f32[128,96]{1,0:T(8,128)S(1)}, f32[128,96]{1,0:T(8,128)S(1)}, u32[]{:S(2)}, u32[]{:S(2)}) collective-permute-start(f32[128,96]{1,0:T(8,128)S(1)} %get-tuple-element.114), channel_id=1, source_target_pairs={{2,0},{3,1},{6,4},{7,5},{10,8},{11,9},{14,12},{15,13},{18,16},{19,... | collective-permute-start | bytes 147464 | tf_op jit(solution)/shard_map/ppermute | solution.py:19
  8.8 10.3 %collective-permute-start = (f32[128,96]{1,0:T(8,128)S(1)}, f32[128,96]{1,0:T(8,128)S(1)}, u32[]{:S(2)}, u32[]{:S(2)}) collective-permute-start(f32[128,96]{1,0:T(8,128)S(1)} %get-tuple-element.115), channel_id=1, source_target_pairs={{0,2},{1,3},{4,6},{5,7},{8,10},{9,11},{12,14},{13,15},{16,18},{17,... | collective-permute-start | bytes 147464 | tf_op jit(solution)/shard_map/ppermute | solution.py:16
  67.4 330.1 %reduce-scatter.2.cloned.1.call-start = ((), (), s32[]{:S(2)}) async-start(), calls=%async_computation.2 | async-start | bytes 12681216 | tf_op jit(solution)/shard_map/reduce_scatter | solution.py:96
Sparse Core Ops, SparseCore 0:
  67.5 23.6 all-gather.1
  297.8 99.6 reduce-scatter.1
where the time goes:
time: 405 us; the launch traced here: 404 us
  matrix products  173 us (43%)
  waiting for transfers between devices  123 us (30%)
  other arithmetic  52.9 us (13%)
  local copies, waits for them, and re-layouts  34.5 us (9%)
  between operations  13.5 us (3%)
  starting transfers between devices  6.39 us (2%)
    conv_general_dilated x8, matrix products, advance(): lax.conv_general_dilated(window[:, None, :], rows_here[:, None, :], (1,),...  168 us
    reduce_scatter x1, waiting for transfers between devices, on_device(): lax.psum_scatter(jnp.transpose(summed[:, :, ::-1], (1, 2, 0)) * norm_scal...  99.8 us
    convert_element_type x1, other arithmetic, on_device(): padded = jnp.where(inside[None, :], whitened_ext, 0.0).astype(jnp.bfloat16)  42.9 us
    all_gather x1, waiting for transfers between devices, on_device(): segment = lax.all_gather(slot_rows, ('chan', 'sub'), axis=0, tiled=True)  23.6 us
    broadcast_in_dim x16, local copies, waits for them, and re-layouts, advance(): window[:, None, :]  9.16 us
    while x1, local copies, waits for them, and re-layouts, correlate(): return lax.fori_loop(0, block_count, advance, start_sum)  9 us
    broadcast_in_dim x16, local copies, waits for them, and re-layouts, advance(): rows_here[:, None, :]  8.59 us
    mul x1, other arithmetic, on_device(): jnp.transpose(summed[:, :, ::-1], (1, 2, 0)) * norm_scale  8.51 us
  transfers between devices with their start and end apart: 4, of which 2 were waited for; matrix products, arithmetic and copies ran while one was open for 1% of the time, Pallas kernels for 0%

commit v1 on v0

v1 whole, which is shorter than its diff:
```python
import functools
import math

import jax
import jax.numpy as jnp
from jax import lax
from jax.experimental import pallas as pl
from jax.experimental.pallas import tpu as pltpu
from jax.sharding import PartitionSpec as P

LAGS = 129
HALF = 64
EDGE = 128
LANES = 128
TB = 128
VMEM_LIMIT = 60 * 1024 * 1024


def whiten_kernel(taps, x_ref, low_ref, high_ref, f_ref, pick_ref, w_ref, slot_ref, xt):
    seg = x_ref.shape[1]
    half_taps = (taps - 1) // 2
    lead = EDGE - half_taps
    xt[0:EDGE, :] = low_ref[...].T
    xt[seg + EDGE : seg + 2 * EDGE, :] = high_ref[...].T

    @pl.loop(0, seg // LANES)
    def _(b):
        t0 = pl.multiple_of(b * LANES, LANES)
        xt[pl.ds(t0 + EDGE, LANES), :] = x_ref[:, pl.ds(t0, LANES)].T

    tall = TB + 8 * (taps // 8)

    @pl.loop(0, seg // TB)
    def _(b):
        t0 = pl.multiple_of(b * TB, TB)
        win = xt[pl.ds(t0 + lead, tall + 8), :]
        acc = jnp.zeros((TB, win.shape[1]), jnp.float32)
        for r in range(8):
            xr = win[r : r + tall]
            for q in range(taps // 8 + 1):
                k = 8 * q + r
                if k < taps:
                    acc = acc + f_ref[k : k + 1, :] * xr[8 * q : 8 * q + TB]
        w = acc.astype(jnp.bfloat16)
        w_ref[pl.ds(t0, TB), :] = w
        slot_ref[:, pl.ds(t0, TB)] = lax.dot_general(
            pick_ref[...], w, (((1,), (1,)), ((), ())), preferred_element_type=jnp.float32
        ).astype(jnp.bfloat16)


def whiten(x, low, high, filters_t, picker):
    chans, seg = x.shape
    slots = picker.shape[0]
    return pl.pallas_call(
        functools.partial(whiten_kernel, filters_t.shape[0]),
        out_shape=(
            jax.ShapeDtypeStruct((seg, chans), jnp.bfloat16),
            jax.ShapeDtypeStruct((slots, seg), jnp.bfloat16),
        ),
        in_specs=[pl.BlockSpec(memory_space=pltpu.VMEM)] * 5,
        out_specs=(pl.BlockSpec(memory_space=pltpu.VMEM),) * 2,
        scratch_shapes=[pltpu.VMEM((seg + 2 * EDGE, chans), jnp.float32)],
        compiler_params=pltpu.CompilerParams(vmem_limit_bytes=VMEM_LIMIT),
        name="whiten",
    )(x, low, high, filters_t, picker)


def chunk_of(total):
    return max(d for d in range(256, 1025, 256) if total % d == 0)


GROUP = 13


def corr_kernel(scale, w_ref, p_ref, out_ref, rhs, xp, acc):
    span, chans = w_ref.shape
    rows = p_ref.shape[0]
    total = rhs.shape[0]
    depth = chunk_of(total)
    rhs[0:span, 0:chans] = w_ref[...]
    rhs[span:total, 0:chans] = jnp.zeros((total - span, chans), jnp.bfloat16)
    rhs[0:HALF, chans:] = jnp.zeros((HALF, chans), jnp.bfloat16)
    rhs[HALF : span + HALF, chans:] = w_ref[...]
    rhs[span + HALF : total, chans:] = jnp.zeros((total - span - HALF, chans), jnp.bfloat16)
    xp[:, 0:EDGE] = jnp.zeros((rows, EDGE), jnp.bfloat16)
    xp[:, EDGE : EDGE + span] = p_ref[...]
    xp[:, EDGE + span :] = jnp.zeros((rows, xp.shape[1] - EDGE - span), jnp.bfloat16)
    acc[...] = jnp.zeros_like(acc)

    @pl.loop(0, total // depth)
    def _(kb):
        k0 = pl.multiple_of(kb * depth, 256)
        xw = xp[:, pl.ds(k0, depth + 128)]
        r = rhs[pl.ds(k0, depth), :]
        for g in range((HALF + 1) // GROUP):
            lhs = jnp.concatenate(
                [xw[:, HALF + i : HALF + i + depth] for i in range(g * GROUP, (g + 1) * GROUP)],
                axis=0,
            )
            here = slice(g * GROUP * rows, (g + 1) * GROUP * rows)
            acc[here, :] += jnp.dot(lhs, r, preferred_element_type=jnp.float32)

    for i in range(HALF + 1):
        if i < HALF:
            out_ref[:, i, :] = acc[i * rows : (i + 1) * rows, 0:chans] * scale
        out_ref[:, i + HALF, :] = acc[i * rows : (i + 1) * rows, chans:] * scale


def correlate(w_full, partners, scale):
    span, chans = w_full.shape
    rows = partners.shape[0]
    total = span + 256
    return pl.pallas_call(
        functools.partial(corr_kernel, scale),
        out_shape=jax.ShapeDtypeStruct((rows, LAGS, chans), jnp.float32),
        in_specs=[pl.BlockSpec(memory_space=pltpu.VMEM)] * 2,
        out_specs=pl.BlockSpec(memory_space=pltpu.VMEM),
        scratch_shapes=[
            pltpu.VMEM((total, 2 * chans), jnp.bfloat16),
            pltpu.VMEM((rows, total + 128), jnp.bfloat16),
            pltpu.VMEM(((HALF + 1) * rows, 2 * chans), jnp.float32),
        ],
        compiler_params=pltpu.CompilerParams(vmem_limit_bytes=VMEM_LIMIT),
        name="correlate",
    )(w_full, partners)


def routing(sources, chan_dev, wide):
    partner_count = sources.shape[0]
    my_block = lax.axis_index(("chan", "sub"))
    owners = sources // chan_dev
    within = sources % chan_dev
    is_mine = owners == my_block
    chan_ids = jnp.arange(wide, dtype=jnp.int32)
    slot_most = min(chan_dev, partner_count // 8)
    order_ids = jnp.arange(partner_count, dtype=jnp.int32)
    same_owner = owners[:, None] == owners[None, :]
    earlier = order_ids[None, :] < order_ids[:, None]
    rank_in = jnp.sum((same_owner & earlier).astype(jnp.int32), axis=1)
    choose = (
        (rank_in[None, :] == jnp.arange(slot_most, dtype=jnp.int32)[:, None]) & is_mine[None, :]
    ).astype(jnp.bfloat16)
    onehot = (within[:, None] == chan_ids[None, :]).astype(jnp.bfloat16)
    picker = jnp.dot(choose, onehot, preferred_element_type=jnp.float32).astype(jnp.bfloat16)
    return picker, owners * slot_most + rank_in


def on_device(traces, filters, sources):
    chan_dev, seg_len = traces.shape
    time_devs = lax.axis_size("tm")
    wide = -(-chan_dev // LANES) * LANES
    picker, slot_id = routing(sources, chan_dev, wide)
    if wide != chan_dev:
        traces = jnp.pad(traces, ((0, wide - chan_dev), (0, 0)))
        filters = jnp.pad(filters, ((0, wide - chan_dev), (0, 0)))
    forward = [(i, i + 1) for i in range(time_devs - 1)]
    backward = [(target, source) for source, target in forward]
    low = lax.ppermute(traces[:, seg_len - EDGE :], "tm", forward)
    high = lax.ppermute(traces[:, :EDGE], "tm", backward)
    w_t, slot_rows = whiten(traces, low, high, filters.T, picker)
    segment = lax.all_gather(slot_rows, ("chan", "sub"), axis=0, tiled=True)
    w_full = lax.all_gather(w_t, "tm", axis=0, tiled=True)
    select = (
        slot_id[:, None] == jnp.arange(segment.shape[0], dtype=jnp.int32)[None, :]
    ).astype(jnp.bfloat16)
    partners = jnp.dot(select, segment, preferred_element_type=jnp.float32).astype(jnp.bfloat16)
    partners = lax.all_to_all(partners, "tm", split_axis=0, concat_axis=1, tiled=True)
    scale = 1.0 / math.sqrt(seg_len * time_devs)
    return correlate(w_full, partners, scale)[:, :, :chan_dev]


def solution(mesh):
    return jax.shard_map(
        on_device,
        mesh=mesh,
        in_specs=(
            P(("groups", "chan", "sub"), "tm"),
            P(("groups", "chan", "sub"), None),
            P("groups"),
        ),
        out_specs=P("tm", None, ("groups", "chan", "sub")),
        check_vma=False,
    )
```

time: 405 us -> 158 us (0.39)
  matrix products: 173 us -> 2.51 us
  waiting for transfers between devices: 123 us -> 39.2 us
  Pallas kernels: 0 us -> 62.3 us
  other arithmetic: 52.9 us -> 1.51 us
  local copies, waits for them, and re-layouts: 34.5 us -> 7.64 us
  blocking collectives: 0 us -> 24.4 us
    conv_general_dilated x8 -> x0, matrix products: 168 us -> none  [advance(): lax.conv_general_dilated(window[:, None, :], rows_here[:, None, :], (1,),...]
    reduce_scatter x1 -> x0, waiting for transfers between devices: 99.8 us -> none  [on_device(): lax.psum_scatter(jnp.transpose(summed[:, :, ::-1], (1, 2, 0)) * norm_scal...]
    pallas_call x0 -> x2, Pallas kernels: none -> 62.3 us  [the longest x1 34.8 us: correlate(): pl.pallas_call(functools.partial(corr_kernel, scale), out_shape=jax.Shape...]
    convert_element_type x1 -> x0, other arithmetic: 42.9 us -> none  [on_device(): padded = jnp.where(inside[None, :], whitened_ext, 0.0).astype(jnp.bfloat16)]
    all_to_all x0 -> x1, blocking collectives: none -> 24.4 us  [on_device(): lax.all_to_all(partners, 'tm', split_axis=0, concat_axis=1, tiled=True)]
    broadcast_in_dim x32 -> x0, local copies, waits for them, and re-layouts: 17.7 us -> none  [the longest x16 9.16 us: advance(): window[:, None, :]]
    all_gather x0 -> x1, waiting for transfers between devices: none -> 14 us  [on_device(): w_full = lax.all_gather(w_t, 'tm', axis=0, tiled=True)]
    while x1 -> x0, local copies, waits for them, and re-layouts: 9 us -> none  [correlate(): return lax.fori_loop(0, block_count, advance, start_sum)]
  transfers between devices with their start and end apart: 4 -> 4, of which waited for: 2 -> 2; matrix products, arithmetic and copies ran while one was open for 1% -> 3% of each run, Pallas kernels for 0% -> 0%
where the time goes in v1:
time: 158 us; the launch traced here: 157 us
  Pallas kernels  62.3 us (39%)
  waiting for transfers between devices  39.2 us (25%)
  blocking collectives  24.4 us (15%)
  between operations  13.5 us (9%)
  local copies, waits for them, and re-layouts  7.64 us (5%)
  starting transfers between devices  6.21 us (4%)
  matrix products  2.51 us (2%)
    pallas_call x1, Pallas kernels, correlate(): pl.pallas_call(functools.partial(corr_kernel, scale), out_shape=jax.Shape...  34.8 us
    pallas_call x1, Pallas kernels, whiten(): pl.pallas_call(functools.partial(whiten_kernel, filters_t.shape[0]), out_...  27.5 us
    all_gather x1, waiting for transfers between devices, on_device(): segment = lax.all_gather(slot_rows, ('chan', 'sub'), axis=0, tiled=True)  24.4 us
    all_to_all x1, blocking collectives, on_device(): lax.all_to_all(partners, 'tm', split_axis=0, concat_axis=1, tiled=True)  24.4 us
    all_gather x1, waiting for transfers between devices, on_device(): w_full = lax.all_gather(w_t, 'tm', axis=0, tiled=True)  14 us
    pallas_call x1, local copies, waits for them, and re-layouts, correlate(): pl.pallas_call(functools.partial(corr_kernel, scale), out_shape=jax.Shape...  5.1 us
    ppermute x1, starting transfers between devices, on_device(): low = lax.ppermute(traces[:, seg_len - EDGE:], 'tm', forward)  4.88 us
  transfers between devices with their start and end apart: 4, of which 2 were waited for; matrix products, arithmetic and copies ran while one was open for 3% of the time, Pallas kernels for 0%

profile of v1, /device:TPU:0, one launch (start us, length us, event | category | flops | bytes accessed | tf_op | source)
XLA Modules:
  0.0 157.2 jit_solution(11495697025814364162)
XLA Ops:
  6.5 0.0 all-gather.5.cloned.1.call-start
  6.5 0.9 fusion.7
  7.4 1.3 collective-permute-start.1
  8.7 4.9 %collective-permute-start = (f32[128,128]{1,0:T(8,128)S(1)}, f32[128,128]{1,0:T(8,128)S(1)}, u32[]{:S(2)}, u32[]{:S(2)}) collective-permute-start(f32[128,128]{1,0:T(8,128)S(1)} %get-tuple-element.12), channel_id=1, source_target_pairs={{0,2},{1,3},{4,6},{5,7},{8,10},{9,11},{12,14},{13,15},{16,18},{17,... | collective-permute-start | bytes 196616 | tf_op jit(solution)/shard_map/ppermute | solution.py:158
  13.6 0.7 and_select_fusion
  14.3 0.7 broadcast_compare_fusion
  14.9 0.2 convert_reduce_fusion
  15.1 0.8 convolution_convert_fusion.1.pick_ref
  15.9 0.0 collective-permute-done.1.high_ref
  15.9 0.0 collective-permute-done.low_ref
  15.9 0.0 copy-start.1
  15.9 0.6 copy-done
  16.5 0.0 copy-done.1
  16.6 27.5 %whiten.1 = (bf16[4096,128]{1,0:T(8,128)(2,1)}, bf16[16,4096]{1,0:T(8,128)(2,1)}) custom-call(f32[128,4096]{1,0:T(8,128)} %x_ref.1, f32[128,128]{1,0:T(8,128)} %copy-done.1, f32[128,128]{1,0:T(8,128)} %copy-done, f32[65,128]{1,0:T(8,128)} %bitcast.9, bf16[16,128]{1,0:T(8,128)(2,1)} %convolution_convert_fusion.1.pick_ref), custom_call_target="tpu_custom_call" | custom-call | tf_op jit(solution)/shard_map/whiten/pallas_call | solution.py:54
  44.1 0.0 all-gather.5.cloned.1.call-update
  44.1 0.0 all-gather.3.cloned.1.call-start
  44.1 0.7 all-gather.3.cloned.1.call-update
  44.8 24.4 %all-gather.5.cloned.1.call-done = bf16[128,4096]{1,0:T(8,128)(2,1)} async-done(((bf16[16,4096]{1,0:T(8,128)(2,1)}), bf16[128,4096]{1,0:T(8,128)(2,1)}) %all-gather.5.cloned.1.call-update) | async-done | bytes 1048592 | tf_op jit(solution)/shard_map/all_gather | solution.py:161
  69.3 1.7 %convolution_convert_fusion = bf16[128,4096]{1,0:T(8,128)(2,1)S(1)} fusion(bf16[128,4096]{1,0:T(8,128)(2,1)} %all-gather.5.cloned.1.call-done, s32[128]{0:T(128)S(1)} %multiply_add_fusion), kind=kOutput, calls=%fused_computation | convolution fusion | flops 134758400 | bytes 2097664 | tf_op jit(solution)/shard_map/dot_general | solution.py:166
  71.0 24.4 %all_to_all.19 = bf16[2,64,4096]{2,1,0:T(8,128)(2,1)S(1)} all-to-all(bf16[2,64,4096]{2,1,0:T(8,128)(2,1)S(1)} %bitcast.6), channel_id=1, replica_groups=mesh['groups'=2,'chan'=4,'tm'=2,'sub'=2] {'tm'}, dimensions={0} | all-to-all | bytes 2097152 | tf_op jit(solution)/shard_map/all_to_all | solution.py:167
  95.3 1.0 copy.10
  96.4 14.0 %all-gather.3.cloned.1.call-done.w_ref = bf16[8192,128]{1,0:T(8,128)(2,1)} async-done(((bf16[4096,128]{1,0:T(8,128)(2,1)}), bf16[8192,128]{1,0:T(8,128)(2,1)}) %all-gather.3.cloned.1.call-update) | async-done | bytes 2097168 | tf_op jit(solution)/shard_map/all_gather | solution.py:162
  110.4 34.8 %correlate.1 = f32[64,129,128]{2,1,0:T(8,128)} custom-call(bf16[8192,128]{1,0:T(8,128)(2,1)} %all-gather.3.cloned.1.call-done.w_ref, bf16[64,8192]{1,0:T(8,128)(2,1)} %bitcast.8), custom_call_target="tpu_custom_call" | custom-call | tf_op jit(solution)/shard_map/correlate/pallas_call | solution.py:113
  145.2 5.1 %copy.9 = f32[64,129,128]{2,0,1:T(8,128)} copy(f32[64,129,128]{2,1,0:T(8,128)} %correlate.1) | data formatting | bytes 8454144 | tf_op jit(solution)/shard_map/correlate/pallas_call | solution.py:113
  (2 shorter events, 0.0 us)
Async XLA Ops:
  6.5 62.7 %all-gather.5.cloned.1.call-start = ((), (), s32[]{:S(2)}) async-start(), calls=%async_computation.2 | async-start | bytes 1179648 | tf_op jit(solution)/shard_map/all_gather | solution.py:161
  7.4 8.5 %collective-permute-start.1 = (f32[128,128]{1,0:T(8,128)S(1)}, f32[128,128]{1,0:T(8,128)S(1)}, u32[]{:S(2)}, u32[]{:S(2)}) collective-permute-start(f32[128,128]{1,0:T(8,128)S(1)} %get-tuple-element.11), channel_id=1, source_target_pairs={{2,0},{3,1},{6,4},{7,5},{10,8},{11,9},{14,12},{15,13},{18,16},{19,... | collective-permute-start | bytes 196616 | tf_op jit(solution)/shard_map/ppermute | solution.py:159
  8.7 7.2 %collective-permute-start = (f32[128,128]{1,0:T(8,128)S(1)}, f32[128,128]{1,0:T(8,128)S(1)}, u32[]{:S(2)}, u32[]{:S(2)}) collective-permute-start(f32[128,128]{1,0:T(8,128)S(1)} %get-tuple-element.12), channel_id=1, source_target_pairs={{0,2},{1,3},{4,6},{5,7},{8,10},{9,11},{12,14},{13,15},{16,18},{17,... | collective-permute-start | bytes 196616 | tf_op jit(solution)/shard_map/ppermute | solution.py:158
  15.9 0.6 copy-start
  15.9 0.6 copy-start.1
  44.1 66.3 %all-gather.3.cloned.1.call-start = ((), (), s32[]{:S(2)}) async-start(), calls=%async_computation.1 | async-start | bytes 3145728 | tf_op jit(solution)/shard_map/all_gather | solution.py:162
Sparse Core Ops, SparseCore 0:
  44.2 25.0 all-gather.4
  70.8 39.5 all-gather.2

commit v2 on v1

--- a/solution.py
+++ b/solution.py
@@ -16,6 +16,18 @@
 VMEM_LIMIT = 60 * 1024 * 1024
 
 
+def filtered(xt, start, f_ref, taps):
+    acc = jnp.zeros((TB, xt.shape[1]), jnp.float32)
+    for r in range(8):
+        part = None
+        for m in range((taps - 1 - r) // 8 + 1):
+            k = 8 * m + r
+            term = f_ref[k : k + 1, :] * xt[pl.ds(start + 8 * m, TB + 8), :]
+            part = term if part is None else part + term
+        acc = acc + part[r : r + TB]
+    return acc
+
+
 def whiten_kernel(taps, x_ref, low_ref, high_ref, f_ref, pick_ref, w_ref, slot_ref, xt):
     seg = x_ref.shape[1]
     half_taps = (taps - 1) // 2
@@ -28,20 +40,10 @@
         t0 = pl.multiple_of(b * LANES, LANES)
         xt[pl.ds(t0 + EDGE, LANES), :] = x_ref[:, pl.ds(t0, LANES)].T
 
-    tall = TB + 8 * (taps // 8)
-
     @pl.loop(0, seg // TB)
     def _(b):
         t0 = pl.multiple_of(b * TB, TB)
-        win = xt[pl.ds(t0 + lead, tall + 8), :]
-        acc = jnp.zeros((TB, win.shape[1]), jnp.float32)
-        for r in range(8):
-            xr = win[r : r + tall]
-            for q in range(taps // 8 + 1):
-                k = 8 * q + r
-                if k < taps:
-                    acc = acc + f_ref[k : k + 1, :] * xr[8 * q : 8 * q + TB]
-        w = acc.astype(jnp.bfloat16)
+        w = filtered(xt, t0 + lead, f_ref, taps).astype(jnp.bfloat16)
         w_ref[pl.ds(t0, TB), :] = w
         slot_ref[:, pl.ds(t0, TB)] = lax.dot_general(
             pick_ref[...], w, (((1,), (1,)), ((), ())), preferred_element_type=jnp.float32
@@ -65,6 +67,157 @@
     )(x, low, high, filters_t, picker)
 
 
+MESH = pl.DeviceIdType.MESH
+CHUNKS = 4
+
+
+def front_kernel(taps, sizes, x_ref, f_ref, pick_ref, w_ref, slot_ref, xt, low, high,
+                 halo_send, halo_recv, w_send, w_recv, slot_send, slot_recv):
+    peers, lines, subs = sizes
+    seg = x_ref.shape[1]
+    width = seg // CHUNKS
+    half_taps = (taps - 1) // 2
+    lead = EDGE - half_taps
+    a, z, s = lax.axis_index("tm"), lax.axis_index("chan"), lax.axis_index("sub")
+    other = lax.rem(a + 1, peers)
+    twin = lax.rem(s + 1, subs)
+
+    barrier = pltpu.get_barrier_semaphore()
+    pl.semaphore_signal(barrier, inc=1, device_id={"tm": other}, device_id_type=MESH)
+    pl.semaphore_signal(barrier, inc=1, device_id={"sub": twin}, device_id_type=MESH)
+    for step in range(1, lines):
+        pl.semaphore_signal(
+            barrier, inc=1, device_id={"chan": lax.rem(z + step, lines)}, device_id_type=MESH
+        )
+    pl.semaphore_wait(barrier, lines + 1)
+
+    def halo(side):
+        src = x_ref.at[:, seg - EDGE : seg] if side == 0 else x_ref.at[:, 0:EDGE]
+        return pltpu.make_async_remote_copy(
+            src_ref=src, dst_ref=(low, high)[side], send_sem=halo_send.at[side],
+            recv_sem=halo_recv.at[side], device_id={"tm": other}, device_id_type=MESH)
+
+    halo(0).start()
+    halo(1).start()
+
+    def w_copy(q, part):
+        view = w_ref.at[part, q * width : (q + 1) * width, :]
+        return pltpu.make_async_remote_copy(
+            src_ref=view, dst_ref=view, send_sem=w_send.at[q], recv_sem=w_recv.at[q],
+            device_id={"tm": other}, device_id_type=MESH)
+
+    def slot_copy(q, part, line, sub, lane, where):
+        view = slot_ref.at[part, line, sub, :, q * width : (q + 1) * width]
+        return pltpu.make_async_remote_copy(
+            src_ref=view, dst_ref=view, send_sem=slot_send.at[q, lane],
+            recv_sem=slot_recv.at[q, part, line, sub], device_id=where, device_id_type=MESH)
+
+    def others():
+        return [lax.rem(z + step, lines) for step in range(1, lines)]
+
+    def spread(q, part, base):
+        copies = [
+            slot_copy(q, part, z, s, base + i, {"chan": line}) for i, line in enumerate(others())
+        ]
+        return copies + [slot_copy(q, part, z, s, base + lines - 1, {"sub": twin})]
+
+    def first(q):
+        return [slot_copy(q, a, z, s, 0, {"tm": other})] + spread(q, a, 1)
+
+    def second(q):
+        return spread(q, other, 1 + lines)
+
+    def third(q):
+        return [
+            slot_copy(q, part, line, s, 1 + 2 * lines + i * (lines - 1) + j, {"sub": twin})
+            for i, part in enumerate((a, other))
+            for j, line in enumerate(others())
+        ]
+
+    def launch(copies):
+        for copy in copies:
+            copy.start()
+
+    def stage_two(q):
+        slot_copy(q, other, z, s, 0, {"tm": other}).wait_recv()
+        launch(second(q))
+
+    def stage_three(q):
+        for part in (a, other):
+            for line in others():
+                slot_copy(q, part, line, s, 0, {"chan": line}).wait_recv()
+        launch(third(q))
+
+    @pl.loop(0, seg // LANES)
+    def _(b):
+        t0 = pl.multiple_of(b * LANES, LANES)
+        xt[pl.ds(t0 + EDGE, LANES), :] = x_ref[:, pl.ds(t0, LANES)].T
+
+    halo(0).wait_recv()
+    halo(1).wait_recv()
+    xt[0:EDGE, :] = jnp.where(a > 0, low[...], 0.0).T
+    xt[seg + EDGE : seg + 2 * EDGE, :] = jnp.where(a < peers - 1, high[...], 0.0).T
+
+    for q in range(CHUNKS):
+
+        @pl.loop(0, width // TB)
+        def _(b):
+            t0 = pl.multiple_of(q * width + b * TB, TB)
+            w_ref[a, pl.ds(t0, TB), :] = filtered(xt, t0 + lead, f_ref, taps).astype(jnp.bfloat16)
+
+        slot_ref[a, z, s, :, q * width : (q + 1) * width] = lax.dot_general(
+            pick_ref[...], w_ref[a, q * width : (q + 1) * width, :],
+            (((1,), (1,)), ((), ())), preferred_element_type=jnp.float32,
+        ).astype(jnp.bfloat16)
+        launch(first(q))
+        w_copy(q, a).start()
+        if q >= 1:
+            stage_two(q - 1)
+        if q >= 2:
+            stage_three(q - 2)
+    stage_two(CHUNKS - 1)
+    stage_three(CHUNKS - 2)
+    stage_three(CHUNKS - 1)
+    halo(0).wait_send()
+    halo(1).wait_send()
+    for q in range(CHUNKS):
+        for part in (a, other):
+            for line in [z] + others():
+                slot_copy(q, part, line, twin, 0, {"sub": twin}).wait_recv()
+        w_copy(q, other).wait_recv()
+        w_copy(q, a).wait_send()
+        for copy in first(q) + second(q) + third(q):
+            copy.wait_send()
+
+
+def front(x, filters_t, picker, sizes):
+    chans, seg = x.shape
+    peers, lines, subs = sizes
+    slots = picker.shape[0]
+    dma = pltpu.SemaphoreType.DMA
+    return pl.pallas_call(
+        functools.partial(front_kernel, filters_t.shape[0], sizes),
+        out_shape=(
+            jax.ShapeDtypeStruct((peers, seg, chans), jnp.bfloat16),
+            jax.ShapeDtypeStruct((peers, lines, subs, slots, seg), jnp.bfloat16),
+        ),
+        in_specs=[pl.BlockSpec(memory_space=pltpu.VMEM)] * 3,
+        out_specs=(pl.BlockSpec(memory_space=pltpu.VMEM),) * 2,
+        scratch_shapes=[
+            pltpu.VMEM((seg + 2 * EDGE, chans), jnp.float32),
+            pltpu.VMEM((chans, EDGE), jnp.float32),
+            pltpu.VMEM((chans, EDGE), jnp.float32),
+            dma((2,)), dma((2,)), dma((CHUNKS,)), dma((CHUNKS,)),
+            dma((CHUNKS, 1 + 2 * lines + 2 * (lines - 1))),
+            dma((CHUNKS, peers, lines, subs)),
+        ],
+        compiler_params=pltpu.CompilerParams(
+            vmem_limit_bytes=VMEM_LIMIT, collective_id=0, has_side_effects=True
+        ),
+        name="front",
+    )(x, filters_t, picker)
+
+
 def chunk_of(total):
     return max(d for d in range(256, 1025, 256) if total % d == 0)
 
@@ -72,19 +225,23 @@
 GROUP = 13
 
 
-def corr_kernel(scale, w_ref, p_ref, out_ref, rhs, xp, acc):
-    span, chans = w_ref.shape
-    rows = p_ref.shape[0]
+def corr_kernel(scale, w_ref, slot_ref, sel_ref, out_ref, rhs, xp, acc):
+    parts, seg, chans = w_ref.shape
+    span = parts * seg
+    rows = sel_ref.shape[0]
     total = rhs.shape[0]
     depth = chunk_of(total)
-    rhs[0:span, 0:chans] = w_ref[...]
     rhs[span:total, 0:chans] = jnp.zeros((total - span, chans), jnp.bfloat16)
     rhs[0:HALF, chans:] = jnp.zeros((HALF, chans), jnp.bfloat16)
-    rhs[HALF : span + HALF, chans:] = w_ref[...]
     rhs[span + HALF : total, chans:] = jnp.zeros((total - span - HALF, chans), jnp.bfloat16)
     xp[:, 0:EDGE] = jnp.zeros((rows, EDGE), jnp.bfloat16)
-    xp[:, EDGE : EDGE + span] = p_ref[...]
     xp[:, EDGE + span :] = jnp.zeros((rows, xp.shape[1] - EDGE - span), jnp.bfloat16)
+    for part in range(parts):
+        rhs[part * seg : (part + 1) * seg, 0:chans] = w_ref[part]
+        rhs[HALF + part * seg : HALF + (part + 1) * seg, chans:] = w_ref[part]
+        xp[:, EDGE + part * seg : EDGE + (part + 1) * seg] = jnp.dot(
+            sel_ref[...], slot_ref[part], preferred_element_type=jnp.float32
+        ).astype(jnp.bfloat16)
     acc[...] = jnp.zeros_like(acc)
 
     @pl.loop(0, total // depth)
@@ -102,18 +259,18 @@
 
     for i in range(HALF + 1):
         if i < HALF:
-            out_ref[:, i, :] = acc[i * rows : (i + 1) * rows, 0:chans] * scale
-        out_ref[:, i + HALF, :] = acc[i * rows : (i + 1) * rows, chans:] * scale
-
-
-def correlate(w_full, partners, scale):
-    span, chans = w_full.shape
-    rows = partners.shape[0]
-    total = span + 256
+            out_ref[i] = acc[i * rows : (i + 1) * rows, 0:chans] * scale
+        out_ref[i + HALF] = acc[i * rows : (i + 1) * rows, chans:] * scale
+
+
+def correlate(w_full, slots, select, scale):
+    parts, seg, chans = w_full.shape
+    rows = select.shape[0]
+    total = parts * seg + 256
     return pl.pallas_call(
         functools.partial(corr_kernel, scale),
-        out_shape=jax.ShapeDtypeStruct((rows, LAGS, chans), jnp.float32),
-        in_specs=[pl.BlockSpec(memory_space=pltpu.VMEM)] * 2,
+        out_shape=jax.ShapeDtypeStruct((LAGS, rows, chans), jnp.float32),
+        in_specs=[pl.BlockSpec(memory_space=pltpu.VMEM)] * 3,
         out_specs=pl.BlockSpec(memory_space=pltpu.VMEM),
         scratch_shapes=[
             pltpu.VMEM((total, 2 * chans), jnp.bfloat16),
@@ -122,7 +279,7 @@
         ],
         compiler_params=pltpu.CompilerParams(vmem_limit_bytes=VMEM_LIMIT),
         name="correlate",
-    )(w_full, partners)
+    )(w_full, slots, select)
 
 
 def routing(sources, chan_dev, wide):
@@ -153,20 +310,33 @@
     if wide != chan_dev:
         traces = jnp.pad(traces, ((0, wide - chan_dev), (0, 0)))
         filters = jnp.pad(filters, ((0, wide - chan_dev), (0, 0)))
-    forward = [(i, i + 1) for i in range(time_devs - 1)]
-    backward = [(target, source) for source, target in forward]
-    low = lax.ppermute(traces[:, seg_len - EDGE :], "tm", forward)
-    high = lax.ppermute(traces[:, :EDGE], "tm", backward)
-    w_t, slot_rows = whiten(traces, low, high, filters.T, picker)
-    segment = lax.all_gather(slot_rows, ("chan", "sub"), axis=0, tiled=True)
-    w_full = lax.all_gather(w_t, "tm", axis=0, tiled=True)
-    select = (
-        slot_id[:, None] == jnp.arange(segment.shape[0], dtype=jnp.int32)[None, :]
-    ).astype(jnp.bfloat16)
-    partners = jnp.dot(select, segment, preferred_element_type=jnp.float32).astype(jnp.bfloat16)
-    partners = lax.all_to_all(partners, "tm", split_axis=0, concat_axis=1, tiled=True)
+    rows = slot_id.shape[0] // time_devs
+    mine = lax.dynamic_slice_in_dim(slot_id, lax.axis_index("tm") * rows, rows, 0)
+    lines, subs = lax.axis_size("chan"), lax.axis_size("sub")
+    slot_count = picker.shape[0] * lines * subs
+    select = (mine[:, None] == jnp.arange(slot_count, dtype=jnp.int32)[None, :]).astype(jnp.bfloat16)
     scale = 1.0 / math.sqrt(seg_len * time_devs)
-    return correlate(w_full, partners, scale)[:, :, :chan_dev]
+    if time_devs == 2 and subs == 2:
+        w_full, slots = front(traces, filters.T, picker, (time_devs, lines, subs))
+        slots = slots.reshape(time_devs, slot_count, seg_len)
+        corr = correlate(w_full, slots, select, scale)
+    else:
+        forward = [(i, i + 1) for i in range(time_devs - 1)]
+        backward = [(target, source) for source, target in forward]
+        low = lax.ppermute(traces[:, seg_len - EDGE :], "tm", forward)
+        high = lax.ppermute(traces[:, :EDGE], "tm", backward)
+        w_t, slot_rows = whiten(traces, low, high, filters.T, picker)
+        segment = lax.all_gather(slot_rows, ("chan", "sub"), axis=0, tiled=True)
+        w_full = lax.all_gather(w_t, "tm", axis=0, tiled=True)
+        every = (
+            slot_id[:, None] == jnp.arange(slot_count, dtype=jnp.int32)[None, :]
+        ).astype(jnp.bfloat16)
+        partners = jnp.dot(every, segment, preferred_element_type=jnp.float32).astype(jnp.bfloat16)
+        partners = lax.all_to_all(partners, "tm", split_axis=0, concat_axis=1, tiled=True)
+        corr = correlate(
+            w_full[None], partners[None], jnp.eye(rows, dtype=jnp.bfloat16), scale
+        )
+    return jnp.transpose(corr, (1, 0, 2))[:, :, :chan_dev]
 
 
 def solution(mesh):

time: 158 us -> 80.3 us (0.51)
  waiting for transfers between devices: 39.2 us -> 0 us
  blocking collectives: 24.4 us -> 0 us
  Pallas kernels: 62.3 us -> 77 us
  between operations: 13.5 us -> 0.02 us
  local copies, waits for them, and re-layouts: 7.64 us -> 0.08 us
  starting transfers between devices: 6.21 us -> 0 us
  matrix products: 2.51 us -> 0.8 us
    all_gather x2 -> x0, waiting for transfers between devices: 38.5 us -> none  [the longest x1 24.4 us: on_device(): segment = lax.all_gather(slot_rows, ('chan', 'sub'), axis=0, tiled=True)]
    all_to_all x1 -> x0, blocking collectives: 24.4 us -> none  [on_device(): lax.all_to_all(partners, 'tm', split_axis=0, concat_axis=1, tiled=True)]
    pallas_call x1, Pallas kernels: 27.5 us -> 43.7 us  [front(): pl.pallas_call(functools.partial(front_kernel, filters_t.shape[0], sizes)...]
    ppermute x2 -> x0, starting transfers between devices: 6.17 us -> none  [the longest x1 4.88 us: on_device(): low = lax.ppermute(traces[:, seg_len - EDGE:], 'tm', forward)]
    pallas_call x1 -> x0, local copies, waits for them, and re-layouts: 5.1 us -> none  [correlate(): pl.pallas_call(functools.partial(corr_kernel, scale), out_shape=jax.Shape...]
    dot_general x1 -> x0, matrix products: 1.7 us -> none  [on_device(): jnp.dot(select, segment, preferred_element_type=jnp.float32)]
  transfers between devices with their start and end apart: 4 -> 0, of which waited for: 2 -> 0; matrix products, arithmetic and copies ran while one was open for 3% -> 0% of each run, Pallas kernels for 0% -> 0%
where the time goes in v2:
time: 80.3 us; the launch traced here: 80.1 us
  Pallas kernels  77 us (96%)
  other arithmetic  2.17 us (3%)
    pallas_call x1, Pallas kernels, front(): pl.pallas_call(functools.partial(front_kernel, filters_t.shape[0], sizes)...  43.7 us
    pallas_call x1, Pallas kernels, correlate(): pl.pallas_call(functools.partial(corr_kernel, scale), out_shape=jax.Shape...  33.4 us

profile of v2, /device:TPU:0, one launch (start us, length us, event | category | flops | bytes accessed | tf_op | source)
XLA Modules:
  0.0 80.1 jit_solution(1231716198994752428)
XLA Ops:
  0.0 0.7 and_select_fusion
  0.7 0.7 broadcast_compare_fusion
  1.3 0.2 convert_reduce_fusion
  1.5 0.1 dynamic_slice.3
  1.6 0.8 convolution_convert_fusion.pick_ref
  2.4 0.7 fusion.2.sel_ref
  3.1 43.7 %front.1 = (bf16[2,4096,128]{2,1,0:T(8,128)(2,1)}, bf16[2,4,2,16,4096]{4,3,2,1,0:T(8,128)(2,1)}) custom-call(f32[128,4096]{1,0:T(8,128)} %x_ref.1, f32[65,128]{1,0:T(8,128)} %bitcast.4, bf16[16,128]{1,0:T(8,128)(2,1)} %convolution_convert_fusion.pick_ref), custom_call_target="tpu_custom_call" | custom-call | tf_op jit(solution)/shard_map/front/pallas_call | solution.py:198
  46.7 33.4 %correlate.1 = f32[129,64,128]{2,1,0:T(8,128)} custom-call(bf16[2,4096,128]{2,1,0:T(8,128)(2,1)} %get-tuple-element.7.w_ref, bf16[2,128,4096]{2,1,0:T(8,128)(2,1)} %bitcast.3, bf16[64,128]{1,0:T(8,128)(2,1)} %fusion.2.sel_ref), custom_call_target="tpu_custom_call" | custom-call | tf_op jit(solution)/shard_map/correlate/pallas_call | solution.py:270
  (1 shorter events, 0.0 us)

commit v3 on v2

--- a/solution.py
+++ b/solution.py
@@ -14,6 +14,7 @@
 LANES = 128
 TB = 128
 VMEM_LIMIT = 60 * 1024 * 1024
+CORR_LIMIT = 40 * 1024 * 1024
 
 
 def filtered(xt, start, f_ref, taps):
@@ -69,9 +70,10 @@
 
 MESH = pl.DeviceIdType.MESH
 CHUNKS = 4
-
-
-def front_kernel(taps, sizes, x_ref, f_ref, pick_ref, w_ref, slot_ref, xt, low, high,
+EARLY = 2
+
+
+def front_kernel(taps, sizes, x_ref, f_ref, pick_ref, w_ref, far_ref, slot_ref, xt, low, high,
                  halo_send, halo_recv, w_send, w_recv, slot_send, slot_recv):
     peers, lines, subs = sizes
     seg = x_ref.shape[1]
@@ -100,11 +102,11 @@
     halo(0).start()
     halo(1).start()
 
-    def w_copy(q, part):
-        view = w_ref.at[part, q * width : (q + 1) * width, :]
+    def w_copy(q):
+        rows = pl.ds(q * width, width)
         return pltpu.make_async_remote_copy(
-            src_ref=view, dst_ref=view, send_sem=w_send.at[q], recv_sem=w_recv.at[q],
-            device_id={"tm": other}, device_id_type=MESH)
+            src_ref=w_ref.at[rows, :], dst_ref=far_ref.at[rows, :], send_sem=w_send.at[q],
+            recv_sem=w_recv.at[q], device_id={"tm": other}, device_id_type=MESH)
 
     def slot_copy(q, part, line, sub, lane, where):
         view = slot_ref.at[part, line, sub, :, q * width : (q + 1) * width]
@@ -163,14 +165,15 @@
         @pl.loop(0, width // TB)
         def _(b):
             t0 = pl.multiple_of(q * width + b * TB, TB)
-            w_ref[a, pl.ds(t0, TB), :] = filtered(xt, t0 + lead, f_ref, taps).astype(jnp.bfloat16)
+            w_ref[pl.ds(t0, TB), :] = filtered(xt, t0 + lead, f_ref, taps).astype(jnp.bfloat16)
 
         slot_ref[a, z, s, :, q * width : (q + 1) * width] = lax.dot_general(
-            pick_ref[...], w_ref[a, q * width : (q + 1) * width, :],
+            pick_ref[...], w_ref[q * width : (q + 1) * width, :],
             (((1,), (1,)), ((), ())), preferred_element_type=jnp.float32,
         ).astype(jnp.bfloat16)
         launch(first(q))
-        w_copy(q, a).start()
+        if q < EARLY:
+            w_copy(q).start()
         if q >= 1:
             stage_two(q - 1)
         if q >= 2:
@@ -184,8 +187,9 @@
         for part in (a, other):
             for line in [z] + others():
                 slot_copy(q, part, line, twin, 0, {"sub": twin}).wait_recv()
-        w_copy(q, other).wait_recv()
-        w_copy(q, a).wait_send()
+        if q < EARLY:
+            w_copy(q).wait_recv()
+            w_copy(q).wait_send()
         for copy in first(q) + second(q) + third(q):
             copy.wait_send()
 
@@ -198,16 +202,17 @@
     return pl.pallas_call(
         functools.partial(front_kernel, filters_t.shape[0], sizes),
         out_shape=(
-            jax.ShapeDtypeStruct((peers, seg, chans), jnp.bfloat16),
+            jax.ShapeDtypeStruct((seg, chans), jnp.bfloat16),
+            jax.ShapeDtypeStruct((seg // CHUNKS * EARLY, chans), jnp.bfloat16),
             jax.ShapeDtypeStruct((peers, lines, subs, slots, seg), jnp.bfloat16),
         ),
         in_specs=[pl.BlockSpec(memory_space=pltpu.VMEM)] * 3,
-        out_specs=(pl.BlockSpec(memory_space=pltpu.VMEM),) * 2,
+        out_specs=(pl.BlockSpec(memory_space=pltpu.VMEM),) * 3,
         scratch_shapes=[
             pltpu.VMEM((seg + 2 * EDGE, chans), jnp.float32),
             pltpu.VMEM((chans, EDGE), jnp.float32),
             pltpu.VMEM((chans, EDGE), jnp.float32),
-            dma((2,)), dma((2,)), dma((CHUNKS,)), dma((CHUNKS,)),
+            dma((2,)), dma((2,)), dma((EARLY,)), dma((EARLY,)),
             dma((CHUNKS, 1 + 2 * lines + 2 * (lines - 1))),
             dma((CHUNKS, peers, lines, subs)),
         ],
@@ -218,68 +223,99 @@
     )(x, filters_t, picker)
 
 
-def chunk_of(total):
-    return max(d for d in range(256, 1025, 256) if total % d == 0)
-
-
 GROUP = 13
 
 
-def corr_kernel(scale, w_ref, slot_ref, sel_ref, out_ref, rhs, xp, acc):
-    parts, seg, chans = w_ref.shape
-    span = parts * seg
+def corr_kernel(scale, first, last, pieces, *refs):
+    base_ref, slot_ref, sel_ref = refs[:3]
+    w_refs = refs[3 : 3 + pieces]
+    rest = refs[3 + pieces :]
+    if not first:
+        prior, rest = rest[0], rest[1:]
+    out_ref, rhs, xp = rest[:3]
+    acc = rest[3] if last else out_ref
+    parts, _, span = slot_ref.shape
+    chans = w_refs[0].shape[1]
+    seg = sum(w_ref.shape[0] for w_ref in w_refs)
     rows = sel_ref.shape[0]
     total = rhs.shape[0]
-    depth = chunk_of(total)
-    rhs[span:total, 0:chans] = jnp.zeros((total - span, chans), jnp.bfloat16)
+    base = pl.multiple_of(base_ref[0] * seg, LANES)
+    rhs[seg:total, 0:chans] = jnp.zeros((total - seg, chans), jnp.bfloat16)
     rhs[0:HALF, chans:] = jnp.zeros((HALF, chans), jnp.bfloat16)
-    rhs[span + HALF : total, chans:] = jnp.zeros((total - span - HALF, chans), jnp.bfloat16)
+    rhs[seg + HALF : total, chans:] = jnp.zeros((total - seg - HALF, chans), jnp.bfloat16)
+    at = 0
+    for w_ref in w_refs:
+        size = w_ref.shape[0]
+        rhs[at : at + size, 0:chans] = w_ref[...]
+        rhs[HALF + at : HALF + at + size, chans:] = w_ref[...]
+        at += size
+    end = EDGE + parts * span
     xp[:, 0:EDGE] = jnp.zeros((rows, EDGE), jnp.bfloat16)
-    xp[:, EDGE + span :] = jnp.zeros((rows, xp.shape[1] - EDGE - span), jnp.bfloat16)
+    xp[:, end:] = jnp.zeros((rows, xp.shape[1] - end), jnp.bfloat16)
     for part in range(parts):
-        rhs[part * seg : (part + 1) * seg, 0:chans] = w_ref[part]
-        rhs[HALF + part * seg : HALF + (part + 1) * seg, chans:] = w_ref[part]
-        xp[:, EDGE + part * seg : EDGE + (part + 1) * seg] = jnp.dot(
+        xp[:, EDGE + part * span : EDGE + (part + 1) * span] = jnp.dot(
             sel_ref[...], slot_ref[part], preferred_element_type=jnp.float32
         ).astype(jnp.bfloat16)
-    acc[...] = jnp.zeros_like(acc)
-
-    @pl.loop(0, total // depth)
-    def _(kb):
-        k0 = pl.multiple_of(kb * depth, 256)
-        xw = xp[:, pl.ds(k0, depth + 128)]
+    acc[...] = jnp.zeros_like(acc) if first else prior[...]
+
+    def step(k0, depth):
+        xw = xp[:, pl.ds(base + k0, depth + 128)]
         r = rhs[pl.ds(k0, depth), :]
         for g in range((HALF + 1) // GROUP):
             lhs = jnp.concatenate(
-                [xw[:, HALF + i : HALF + i + depth] for i in range(g * GROUP, (g + 1) * GROUP)],
-                axis=0,
+                [shifted(xw, HALF + i, depth) for i in range(g * GROUP, (g + 1) * GROUP)], axis=0
             )
             here = slice(g * GROUP * rows, (g + 1) * GROUP * rows)
             acc[here, :] += jnp.dot(lhs, r, preferred_element_type=jnp.float32)
 
-    for i in range(HALF + 1):
-        if i < HALF:
-            out_ref[i] = acc[i * rows : (i + 1) * rows, 0:chans] * scale
-        out_ref[i + HALF] = acc[i * rows : (i + 1) * rows, chans:] * scale
-
-
-def correlate(w_full, slots, select, scale):
-    parts, seg, chans = w_full.shape
+    @pl.loop(0, total // DEPTH)
+    def _(kb):
+        step(pl.multiple_of(kb * DEPTH, 256), DEPTH)
+
+    if total % DEPTH:
+        step(total // DEPTH * DEPTH, total % DEPTH)
+    if last:
+        for i in range(HALF + 1):
+            if i < HALF:
+                out_ref[i] = acc[i * rows : (i + 1) * rows, 0:chans] * scale
+            out_ref[i + HALF] = acc[i * rows : (i + 1) * rows, chans:] * scale
+
+
+DEPTH = 768
+
+
+def shifted(xw, by, depth):
+    return xw[:, by : by + depth]
+
+
+def correlate(base, slots, select, w_pieces, prior, last, scale):
+    chans = w_pieces[0].shape[1]
+    seg = sum(piece.shape[0] for piece in w_pieces)
     rows = select.shape[0]
-    total = parts * seg + 256
+    whole = slots.shape[0] * slots.shape[2]
+    total = seg + 256
+    held = ((HALF + 1) * rows, 2 * chans)
+    first = prior is None
+    vmem = pl.BlockSpec(memory_space=pltpu.VMEM)
+    extra = [] if first else [prior]
     return pl.pallas_call(
-        functools.partial(corr_kernel, scale),
-        out_shape=jax.ShapeDtypeStruct((LAGS, rows, chans), jnp.float32),
-        in_specs=[pl.BlockSpec(memory_space=pltpu.VMEM)] * 3,
-        out_specs=pl.BlockSpec(memory_space=pltpu.VMEM),
+        functools.partial(corr_kernel, scale, first, last, len(w_pieces)),
+        out_shape=jax.ShapeDtypeStruct((LAGS, rows, chans) if last else held, jnp.float32),
+        in_specs=[pl.BlockSpec(memory_space=pltpu.SMEM)]
+        + [vmem] * (2 + len(w_pieces) + len(extra)),
+        out_specs=vmem,
         scratch_shapes=[
             pltpu.VMEM((total, 2 * chans), jnp.bfloat16),
-            pltpu.VMEM((rows, total + 128), jnp.bfloat16),
-            pltpu.VMEM(((HALF + 1) * rows, 2 * chans), jnp.float32),
-        ],
-        compiler_params=pltpu.CompilerParams(vmem_limit_bytes=VMEM_LIMIT),
-        name="correlate",
-    )(w_full, slots, select)
+            pltpu.VMEM((rows, whole + 512), jnp.bfloat16),
+        ]
+        + ([pltpu.VMEM(held, jnp.float32)] if last else []),
+        compiler_params=pltpu.CompilerParams(vmem_limit_bytes=CORR_LIMIT),
+        cost_estimate=pl.CostEstimate(
+            flops=2 * total * held[0] * held[1], bytes_accessed=12 * held[0] * held[1],
+            transcendentals=0,
+        ),
+        name="correlate_last" if last else "correlate_first",
+    )(base, slots, select, *w_pieces, *extra)
 
 
 def routing(sources, chan_dev, wide):
@@ -317,9 +353,12 @@
     select = (mine[:, None] == jnp.arange(slot_count, dtype=jnp.int32)[None, :]).astype(jnp.bfloat16)
     scale = 1.0 / math.sqrt(seg_len * time_devs)
     if time_devs == 2 and subs == 2:
-        w_full, slots = front(traces, filters.T, picker, (time_devs, lines, subs))
+        w_near, w_far, slots = front(traces, filters.T, picker, (time_devs, lines, subs))
+        late = lax.ppermute(w_near[w_far.shape[0] :], "tm", [(0, 1), (1, 0)])
         slots = slots.reshape(time_devs, slot_count, seg_len)
-        corr = correlate(w_full, slots, select, scale)
+        here = lax.axis_index("tm").astype(jnp.int32).reshape(1)
+        held = correlate(here, slots, select, [w_near], None, False, scale)
+        corr = correlate(1 - here, slots, select, [w_far, late], held, True, scale)
     else:
         forward = [(i, i + 1) for i in range(time_devs - 1)]
         backward = [(target, source) for source, target in forward]
@@ -334,7 +373,8 @@
         partners = jnp.dot(every, segment, preferred_element_type=jnp.float32).astype(jnp.bfloat16)
         partners = lax.all_to_all(partners, "tm", split_axis=0, concat_axis=1, tiled=True)
         corr = correlate(
-            w_full[None], partners[None], jnp.eye(rows, dtype=jnp.bfloat16), scale
+            jnp.zeros((1,), jnp.int32), partners[None], jnp.eye(rows, dtype=jnp.bfloat16),
+            [w_full], None, True, scale,
         )
     return jnp.transpose(corr, (1, 0, 2))[:, :, :chan_dev]
 

time: 80.3 us -> 81.3 us (1.012)
  local copies, waits for them, and re-layouts: 0.08 us -> 3.97 us
  Pallas kernels: 77 us -> 74.5 us
    unnamed x0 -> x8, local copies, waits for them, and re-layouts: none -> 2.82 us
    pallas_call x1, Pallas kernels: 43.7 us -> 41.8 us  [front(): pl.pallas_call(functools.partial(front_kernel, filters_t.shape[0], sizes)...]
    slice x0 -> x1, local copies, waits for them, and re-layouts: none -> 1.08 us  [on_device(): late = lax.ppermute(w_near[w_far.shape[0]:], 'tm', [(0, 1), (1, 0)])]
    pallas_call x1 -> x2, Pallas kernels: 33.4 us -> 32.7 us  [correlate(): pl.pallas_call(functools.partial(corr_kernel, scale, first, last, len(w_p...]
  transfers between devices with their start and end apart: 0 -> 1, of which waited for: 0 -> 0; matrix products, arithmetic and copies ran while one was open for 0% -> 0% of each run, Pallas kernels for 0% -> 19%
where the time goes in v3:
time: 81.3 us; the launch traced here: 81 us
  Pallas kernels  74.5 us (92%)
  local copies, waits for them, and re-layouts  3.97 us (5%)
  other arithmetic  1.58 us (2%)
    pallas_call x1, Pallas kernels, front(): pl.pallas_call(functools.partial(front_kernel, filters_t.shape[0], sizes)...  41.8 us
    pallas_call x2, Pallas kernels, correlate(): pl.pallas_call(functools.partial(corr_kernel, scale, first, last, len(w_p...  32.7 us
    unnamed x8, local copies, waits for them, and re-layouts  2.82 us
  transfers between devices with their start and end apart: 1, of which 0 were waited for; matrix products, arithmetic and copies ran while one was open for 0% of the time, Pallas kernels for 19%

profile of v3, /device:TPU:0, one launch (start us, length us, event | category | flops | bytes accessed | tf_op | source)
XLA Modules:
  0.0 81.0 jit_solution(3100088282024619754)
XLA Ops:
  0.0 0.7 and_select_fusion
  0.7 0.7 broadcast_compare_fusion
  1.3 0.2 convert_reduce_fusion
  1.5 0.8 convolution_convert_fusion.pick_ref
  2.3 41.8 %front.1 = (bf16[4096,128]{1,0:T(8,128)(2,1)}, bf16[2048,128]{1,0:T(8,128)(2,1)}, bf16[2,4,2,16,4096]{4,3,2,1,0:T(8,128)(2,1)}) custom-call(f32[128,4096]{1,0:T(8,128)} %x_ref.1, f32[65,128]{1,0:T(8,128)} %bitcast.6, bf16[16,128]{1,0:T(8,128)(2,1)} %convolution_convert_fusion.pick_ref), custom_call_target="tpu_custom_call" | custom-call | tf_op jit(solution)/shard_map/front/pallas_call | solution.py:202
  44.2 1.1 %slice.3 = bf16[2048,128]{1,0:T(8,128)(2,1)S(1)} slice(bf16[4096,128]{1,0:T(8,128)(2,1)} %get-tuple-element.10.refs_3_), slice={[2048:4096], [0:128]} | slice | bytes 1048576 | tf_op jit(solution)/shard_map/slice | solution.py:357
  45.2 0.1 collective-permute-start
  45.3 0.1 dynamic_slice.3
  45.4 0.1 fusion.2.refs_2_
  45.5 0.0 copy-start
  45.5 1.2 %copy-done = bf16[4096,128]{1,0:T(8,128)(2,1)S(1)} copy-done((bf16[4096,128]{1,0:T(8,128)(2,1)S(1)}, bf16[4096,128]{1,0:T(8,128)(2,1)}, u32[]{:S(2)}) %copy-start) | copy-done | bytes 1048600
  46.7 0.0 copy-start.1
  46.7 1.6 %copy-done.1 = bf16[2,4,2,16,4096]{4,3,2,1,0:T(8,128)(2,1)S(1)} copy-done((bf16[2,4,2,16,4096]{4,3,2,1,0:T(8,128)(2,1)S(1)}, bf16[2,4,2,16,4096]{4,3,2,1,0:T(8,128)(2,1)}, u32[]{:S(2)}) %copy-start.1) | copy-done | bytes 2097176
  48.3 0.0 copy-start.2
  48.3 0.0 copy-start.3
  48.3 15.5 %correlate_first.1.refs_5_ = f32[4160,256]{1,0:T(8,128)S(1)} custom-call(s32[1]{0:T(128)} %bitcast.refs_0_, bf16[2,128,4096]{2,1,0:T(8,128)(2,1)S(1)} %bitcast.4, bf16[64,128]{1,0:T(8,128)(2,1)S(1)} %fusion.2.refs_2_, bf16[4096,128]{1,0:T(8,128)(2,1)S(1)} %copy-done), custom_call_target="tpu_custom_call" | custom-call | flops 9269411840 | bytes 12779520 | tf_op jit(solution)/shard_map/correlate_first/pallas_call | solution.py:301
  63.8 0.0 collective-permute-done.refs_4_
  63.8 0.0 copy-done.2
  63.8 0.0 copy-done.3
  63.8 17.2 %correlate_last.1 = f32[129,64,128]{2,1,0:T(8,128)} custom-call(s32[1]{0:T(128)S(6)} %sub.9.refs_0_, bf16[2,128,4096]{2,1,0:T(8,128)(2,1)S(1)} %bitcast.5, bf16[64,128]{1,0:T(8,128)(2,1)S(1)} %fusion.2.refs_2_, bf16[2048,128]{1,0:T(8,128)(2,1)S(1)} %copy-done.3, bf16[2048,128]{1,0:T(8,128)(2,1)S(1)} %collective-permute-done.refs_4_, ...), custom_call_target="tpu_custom_call" | custom-call | flops 9269411840 | bytes 12779520 | tf_op jit(solution)/shard_map/correlate_last/pallas_call | solution.py:301
  (1 shorter events, 0.0 us)
Async XLA Ops:
  45.2 18.5 %collective-permute-start = (bf16[2048,128]{1,0:T(8,128)(2,1)S(1)}, bf16[2048,128]{1,0:T(8,128)(2,1)S(1)}, u32[]{:S(2)}, u32[]{:S(2)}) collective-permute-start(bf16[2048,128]{1,0:T(8,128)(2,1)S(1)} %slice.3), channel_id=1, source_target_pairs={{0,2},{2,0},{1,3},{3,1},{4,6},{6,4},{5,7},{7,5},{8,10},{10,8},{9,1... | collective-permute-start | bytes 1572872 | tf_op jit(solution)/shard_map/ppermute | solution.py:357
  45.5 1.2 %copy-start = (bf16[4096,128]{1,0:T(8,128)(2,1)S(1)}, bf16[4096,128]{1,0:T(8,128)(2,1)}, u32[]{:S(2)}) copy-start(bf16[4096,128]{1,0:T(8,128)(2,1)} %get-tuple-element.10.refs_3_) | copy-start | bytes 3145732
  46.7 1.6 %copy-start.1 = (bf16[2,4,2,16,4096]{4,3,2,1,0:T(8,128)(2,1)S(1)}, bf16[2,4,2,16,4096]{4,3,2,1,0:T(8,128)(2,1)}, u32[]{:S(2)}) copy-start(bf16[2,4,2,16,4096]{4,3,2,1,0:T(8,128)(2,1)} %get-tuple-element.8) | copy-start | bytes 6291460
  48.3 15.5 %copy-start.2 = (bf16[2,4,2,16,4096]{4,3,2,1,0:T(8,128)(2,1)S(1)}, bf16[2,4,2,16,4096]{4,3,2,1,0:T(8,128)(2,1)}, u32[]{:S(2)}) copy-start(bf16[2,4,2,16,4096]{4,3,2,1,0:T(8,128)(2,1)} %get-tuple-element.8) | copy-start | bytes 6291460
  48.3 15.5 %copy-start.3 = (bf16[2048,128]{1,0:T(8,128)(2,1)S(1)}, bf16[2048,128]{1,0:T(8,128)(2,1)}, u32[]{:S(2)}) copy-start(bf16[2048,128]{1,0:T(8,128)(2,1)} %get-tuple-element.9.refs_3_) | copy-start | bytes 1572868

commit v4 on v2

--- a/solution.py
+++ b/solution.py
@@ -251,7 +251,10 @@
         r = rhs[pl.ds(k0, depth), :]
         for g in range((HALF + 1) // GROUP):
             lhs = jnp.concatenate(
-                [xw[:, HALF + i : HALF + i + depth] for i in range(g * GROUP, (g + 1) * GROUP)],
+                [
+                    pltpu.roll(xw, depth + LANES - HALF - i, 1)[:, :depth]
+                    for i in range(g * GROUP, (g + 1) * GROUP)
+                ],
                 axis=0,
             )
             here = slice(g * GROUP * rows, (g + 1) * GROUP * rows)

time: 80.3 us -> 77.1 us (0.960)
  Pallas kernels: 77 us -> 73.8 us
    pallas_call x1, Pallas kernels: 33.4 us -> 30.2 us  [correlate(): pl.pallas_call(functools.partial(corr_kernel, scale), out_shape=jax.Shape...]
where the time goes in v4:
time: 77.1 us; the launch traced here: 76.9 us
  Pallas kernels  73.8 us (96%)
  other arithmetic  2.17 us (3%)
  matrix products  0.8 us (1%)
    pallas_call x1, Pallas kernels, front(): pl.pallas_call(functools.partial(front_kernel, filters_t.shape[0], sizes)...  43.7 us
    pallas_call x1, Pallas kernels, correlate(): pl.pallas_call(functools.partial(corr_kernel, scale), out_shape=jax.Shape...  30.2 us

profile of v4, /device:TPU:0, one launch (start us, length us, event | category | flops | bytes accessed | tf_op | source)
XLA Modules:
  0.0 76.9 jit_solution(16302192251123750982)
XLA Ops:
  0.0 0.7 and_select_fusion
  0.7 0.7 broadcast_compare_fusion
  1.3 0.2 convert_reduce_fusion
  1.5 0.1 dynamic_slice.3
  1.6 0.8 %convolution_convert_fusion.pick_ref = bf16[16,128]{1,0:T(8,128)(2,1)} fusion(s32[128]{0:T(128)S(1)} %and_select_fusion, s32[128]{0:T(128)S(1)} %convert_reduce_fusion, pred[128]{0:T(512)(128)(4,1)S(1)} %get-tuple-element.9), kind=kOutput, calls=%fused_computation | convolution fusion | flops 546816 | bytes 5248 | tf_op jit(solution)/shard_map/dot_general | solution.py:304
  2.4 0.7 fusion.2.sel_ref
  3.1 43.7 %front.1 = (bf16[2,4096,128]{2,1,0:T(8,128)(2,1)}, bf16[2,4,2,16,4096]{4,3,2,1,0:T(8,128)(2,1)}) custom-call(f32[128,4096]{1,0:T(8,128)} %x_ref.1, f32[65,128]{1,0:T(8,128)} %bitcast.4, bf16[16,128]{1,0:T(8,128)(2,1)} %convolution_convert_fusion.pick_ref), custom_call_target="tpu_custom_call" | custom-call | tf_op jit(solution)/shard_map/front/pallas_call | solution.py:198
  46.7 30.2 %correlate.1 = f32[129,64,128]{2,1,0:T(8,128)} custom-call(bf16[2,4096,128]{2,1,0:T(8,128)(2,1)} %get-tuple-element.7.w_ref, bf16[2,128,4096]{2,1,0:T(8,128)(2,1)} %bitcast.3, bf16[64,128]{1,0:T(8,128)(2,1)} %fusion.2.sel_ref), custom_call_target="tpu_custom_call" | custom-call | tf_op jit(solution)/shard_map/correlate/pallas_call | solution.py:273
  (1 shorter events, 0.0 us)
